TPU v7x, 32 devices: a whole 2x2x4 slice. The times are simulated.
32 devices in a mesh: block: 4 (over y, x), dp: 8 (over z, core).
Axes of the slice: x: 2, y: 2, z: 4, core: 2. Of those that a mesh axis runs over, the one named last changes fastest.
Arguments:
- tokens: bfloat16 [2048, 16384], P('dp', 'block'), may hold values from -6 to 6
- first_up: bfloat16 [128, 128, 128], P('block'), may hold values from -0.5 to 0.5
- second_up: bfloat16 [128, 128, 512], P('block'), may hold values from -0.5 to 0.5
- first_down: bfloat16 [128, 512, 128], P('block'), may hold values from -0.25 to 0.25
- second_down: bfloat16 [128, 128, 128], P('block'), may hold values from -0.5 to 0.5
- cotangent: bfloat16 [2048, 16384], P('dp', 'block'), may hold values from -6 to 6
Outputs:
- output: bfloat16 [2048, 16384], P('dp', 'block')
- input_grad: bfloat16 [2048, 16384], P('dp', 'block')
- grad_first_up: float32 [128, 128, 128], P('block', 'dp')
- grad_second_up: float32 [128, 128, 512], P('block', 'dp')
- grad_first_down: float32 [128, 512, 128], P('block', 'dp')
- grad_second_down: float32 [128, 128, 128], P('block', 'dp')
All inputs are finite; a program needn't handle non-finite values.
Results may differ from a plain program's by a relative error of at most 0.0071.
Values may be sent and summed in bfloat16 or wider, within the bound.
No kernel may reach another device: no remote copies, remote signals or barrier semaphores. Data moves between devices by JAX's collectives and lax.ppermute only.
A program may use at most 192 MiB of HBM per device.

v0:
```python
import math
import jax
import jax.numpy as jnp
from jax import lax
from jax.sharding import PartitionSpec as P


def gelu_pair(values):
    factor = math.sqrt(2.0 / math.pi)
    tanh_part = jnp.tanh(factor * (values + 0.044715 * values * values * values))
    active = 0.5 * values * (1.0 + tanh_part)
    slope_term = 0.5 * (1.0 + tanh_part) + 0.5 * values * (1.0 - tanh_part * tanh_part) * factor * (
        1.0 + 3.0 * 0.044715 * values * values
    )
    return (active, slope_term)


def pack_blocks(array, groups):
    count, local_blocks, width = array.shape
    return (
        array.reshape(count, local_blocks, groups, width // groups)
        .transpose(0, 2, 1, 3)
        .reshape(count, groups, -1)
    )


def unpack_blocks(array, groups, local_blocks):
    count = array.shape[0]
    return (
        array.reshape(count, groups, local_blocks, -1)
        .transpose(0, 2, 1, 3)
        .reshape(count, local_blocks, -1)
    )


def local(tokens, first_up, second_up, first_down, second_down, cotangent):
    narrow = jnp.bfloat16
    wide = jnp.float32
    groups = lax.axis_size("block")
    local_blocks = first_up.shape[0]
    width = first_up.shape[1]
    local_feats = width // groups
    count = tokens.shape[0]
    inputs_b = tokens.reshape(count, local_blocks, width)
    cot_b = cotangent.reshape(count, local_blocks, width)
    mixed_in = jnp.einsum("tbi,bij->tbj", inputs_b, first_up, preferred_element_type=wide).astype(
        narrow
    )
    packed_in = pack_blocks(mixed_in, groups)
    piece = lax.all_to_all(packed_in, "block", split_axis=1, concat_axis=1, tiled=True)
    mixed_piece = piece.reshape(piece.shape[0], -1, local_feats)
    before = jnp.einsum("tbj,jbk->tjk", mixed_piece, second_up, preferred_element_type=wide)
    active, slope_term = gelu_pair(before)
    active_b = active.astype(narrow)
    out_j = jnp.einsum("tjk,jkb->tbj", active_b, first_down, preferred_element_type=wide).astype(
        narrow
    )
    mixed_out = unpack_blocks(
        lax.all_to_all(
            out_j.reshape(count, groups, -1), "block", split_axis=1, concat_axis=1, tiled=True
        ),
        groups,
        local_blocks,
    )
    result = jnp.einsum("tbj,bji->tbi", mixed_out, second_down, preferred_element_type=wide).astype(
        narrow
    )
    g_sd = jnp.einsum("tbj,tbi->bji", mixed_out, cot_b, preferred_element_type=wide)
    back_out = jnp.einsum("tbi,bji->tbj", cot_b, second_down, preferred_element_type=wide).astype(
        narrow
    )
    back_j = lax.all_to_all(
        pack_blocks(back_out, groups), "block", split_axis=1, concat_axis=1, tiled=True
    ).reshape(count, -1, local_feats)
    g_fd = jnp.einsum("tjk,tbj->jkb", active_b, back_j, preferred_element_type=wide)
    back_pre = (
        jnp.einsum("tbj,jkb->tjk", back_j, first_down, preferred_element_type=wide) * slope_term
    ).astype(narrow)
    g_su = jnp.einsum("tbj,tjk->jbk", mixed_piece, back_pre, preferred_element_type=wide)
    back_in_j = jnp.einsum("tjk,jbk->tbj", back_pre, second_up, preferred_element_type=wide).astype(
        narrow
    )
    back_in = unpack_blocks(
        lax.all_to_all(
            back_in_j.reshape(count, groups, -1), "block", split_axis=1, concat_axis=1, tiled=True
        ),
        groups,
        local_blocks,
    )
    g_fu = jnp.einsum("tbi,tbj->bij", inputs_b, back_in, preferred_element_type=wide)
    input_rows = jnp.einsum("tbj,bij->tbi", back_in, first_up, preferred_element_type=wide).astype(
        narrow
    )
    red_fu, red_su, red_fd, red_sd = (
        lax.psum_scatter(g_fu, "dp", scatter_dimension=1, tiled=True),
        lax.psum_scatter(g_su, "dp", scatter_dimension=1, tiled=True),
        lax.psum_scatter(g_fd, "dp", scatter_dimension=1, tiled=True),
        lax.psum_scatter(g_sd, "dp", scatter_dimension=1, tiled=True),
    )
    return (
        result.reshape(count, -1),
        input_rows.reshape(count, -1),
        red_fu,
        red_su,
        red_fd,
        red_sd,
    )


def solution(mesh):
    placed = (
        P("dp", "block"),
        P("block", None, None),
        P("block", None, None),
        P("block", None, None),
        P("block", None, None),
        P("dp", "block"),
    )
    return jax.shard_map(
        local,
        mesh=mesh,
        in_specs=placed,
        out_specs=(
            P("dp", "block"),
            P("dp", "block"),
            P("block", "dp", None),
            P("block", "dp", None),
            P("block", "dp", None),
            P("block", "dp", None),
        ),
        check_vma=False,
    )
```

profile of v0, /device:TPU:0, one launch (start us, length us, event | category | flops | bytes accessed | tf_op | source)
XLA Modules:
  0.0 411.0 jit_solution(18226913873195435735)
XLA Ops:
  7.2 0.0 copy-start
  7.2 2.8 fusion.18
  10.0 1.5 copy.59
  11.5 0.0 copy-start.6
  11.5 5.3 %all-to-all-start.2 = ((bf16[256,4,1024]{0,2,1:T(8,128)(2,1)}), bf16[256,4,1024]{0,2,1:T(8,128)(2,1)}, u32[]{:S(2)}, u32[]{:S(2)}) async-start(bf16[256,4,1024]{0,2,1:T(8,128)(2,1)} %bitcast.103), calls=%async_computation.2 | async-start | bytes 4194304 | tf_op jit(solution)/shard_map/all_to_all | solution.py:72
  16.8 0.0 copy-done
  16.8 0.0 copy-done.6
  16.8 0.8 fusion.15
  17.6 1.5 copy.51
  19.1 23.4 %all-to-all-done.2 = bf16[256,4,1024]{0,2,1:T(8,128)(2,1)} async-done(((bf16[256,4,1024]{0,2,1:T(8,128)(2,1)}), bf16[256,4,1024]{0,2,1:T(8,128)(2,1)}, u32[]{:S(2)}, u32[]{:S(2)}) %all-to-all-start.2) | async-done | bytes 2097184 | tf_op jit(solution)/shard_map/all_to_all | solution.py:72
  42.5 4.5 %all-to-all-start = ((bf16[256,4,1024]{0,2,1:T(8,128)(2,1)}), bf16[256,4,1024]{0,2,1:T(8,128)(2,1)}, u32[]{:S(2)}, u32[]{:S(2)}) async-start(bf16[256,4,1024]{0,2,1:T(8,128)(2,1)} %bitcast.102), calls=%async_computation | async-start | bytes 4194304 | tf_op jit(solution)/shard_map/all_to_all | solution.py:50
  47.1 0.0 reduce-scatter.5.cloned.1.call-start
  47.1 4.5 %copy.60 = bf16[256,128,32]{1,0,2:T(8,128)(2,1)} copy(bf16[256,128,32]{0,2,1:T(8,128)(2,1)} %bitcast.17) | data formatting | bytes 4194304 | tf_op jit(solution)/shard_map/reshape | solution.py:74
  51.6 20.1 %all-to-all-done = bf16[256,4,1024]{0,2,1:T(8,128)(2,1)} async-done(((bf16[256,4,1024]{0,2,1:T(8,128)(2,1)}), bf16[256,4,1024]{0,2,1:T(8,128)(2,1)}, u32[]{:S(2)}, u32[]{:S(2)}) %all-to-all-start) | async-done | bytes 2097184 | tf_op jit(solution)/shard_map/all_to_all | solution.py:50
  71.7 0.0 copy-start.4
  71.7 14.1 %multiply_convert_fusion = (bf16[256,32,512]{2,0,1:T(8,128)(2,1)}, f32[32,256,512]{2,1,0:T(8,128)}) fusion(bf16[32,128,512]{2,1,0:T(8,128)(2,1)} %param.8, bf16[256,128,32]{0,2,1:T(8,128)(2,1)} %bitcast.4), kind=kOutput, calls=%fused_computation.10 | convolution fusion | flops 1111490560 | bytes 31457280 | tf_op jit(solution)/shard_map/tbj,jbk->tjk/dot_general | solution.py:52
  85.8 0.0 copy-done.4
  85.8 0.0 copy-start.5
  85.8 17.3 %fusion.6 = bf16[256,32,512]{2,0,1:T(8,128)(2,1)} fusion(f32[32,256,512]{2,1,0:T(8,128)} %get-tuple-element.25, bf16[256,128,32]{1,0,2:T(8,128)(2,1)S(1)} %copy-done.4, bf16[32,512,128]{2,1,0:T(8,128)(2,1)} %param.9), kind=kOutput, calls=%fused_computation.8 | convolution fusion | flops 1153433600 | bytes 31457280 | tf_op jit(solution)/shard_map/tbj,jkb->tjk/dot_general | solution.py:77
  103.1 0.0 copy-done.5
  103.1 6.3 %convert_bitcast_fusion = bf16[256,128,32]{0,1,2:T(8,128)(2,1)S(1)} fusion(bf16[256,32,512]{2,0,1:T(8,128)(2,1)} %fusion.6, bf16[32,128,512]{2,1,0:T(8,128)(2,1)S(1)} %copy-done.5), kind=kOutput, calls=%fused_computation.19 | convolution fusion | flops 1074790400 | bytes 14680064 | tf_op jit(solution)/shard_map/tjk,jbk->tbj/dot_general | solution.py:80
  109.4 1.2 copy.61
  110.6 27.4 %all_to_all.20 = bf16[256,4,1024]{0,2,1:T(8,128)(2,1)S(1)} all-to-all(bf16[256,4,1024]{0,2,1:T(8,128)(2,1)S(1)} %bitcast.104), channel_id=1, replica_groups=mesh['block'=4,'dp'=8] {'block'}, dimensions={1} | all-to-all | bytes 4194304 | tf_op jit(solution)/shard_map/all_to_all | solution.py:84
  137.9 0.2 copy.62
  138.2 0.0 copy-start.1
  138.2 1.4 copy-done.1
  139.5 2.1 fusion.29
  141.6 3.2 copy.65
  144.8 0.0 reduce-scatter.5.cloned.1.call-update
  144.8 0.0 reduce-scatter.11.cloned.1.call-start
  144.8 8.8 %convert_bitcast_fusion.1 = bf16[256,128,32]{0,1,2:T(8,128)(2,1)} fusion(bf16[256,32,512]{2,0,1:T(8,128)(2,1)} %get-tuple-element.24, bf16[32,512,128]{2,1,0:T(8,128)(2,1)} %param.9), kind=kOutput, calls=%fused_computation.20 | convolution fusion | flops 1074790400 | bytes 14680064 | tf_op jit(solution)/shard_map/tjk,jkb->tbj/dot_general | solution.py:55
  153.6 2.8 copy.54
  156.4 26.0 %all_to_all.21 = bf16[256,4,1024]{0,2,1:T(8,128)(2,1)S(1)} all-to-all(bf16[256,4,1024]{0,2,1:T(8,128)(2,1)S(1)} %bitcast.106), channel_id=1, replica_groups=mesh['block'=4,'dp'=8] {'block'}, dimensions={1} | all-to-all | bytes 4194304 | tf_op jit(solution)/shard_map/all_to_all | solution.py:59
  182.4 0.0 copy-start.3
  182.4 0.2 copy.55
  182.6 0.0 copy-start.2
  182.7 1.3 copy-done.2
  184.0 0.8 copy-done.3
  184.7 2.0 fusion.7
  186.8 0.0 reduce-scatter.11.cloned.1.call-update
  186.8 0.0 reduce-scatter.7.cloned.1.call-start
  186.8 10.2 %fusion.27 = f32[32,128,512]{2,1,0:T(8,128)} fusion(bf16[256,32,512]{2,0,1:T(8,128)(2,1)} %fusion.6, bf16[256,128,32]{0,2,1:T(8,128)(2,1)} %bitcast.4), kind=kOutput, calls=%fused_computation.31 | convolution fusion | flops 1073741824 | bytes 18874368 | tf_op jit(solution)/shard_map/tbj,tjk->jbk/dot_general | solution.py:79
  197.0 0.0 reduce-scatter.7.cloned.1.call-update
  197.0 0.3 reduce-scatter.9.cloned.1.call-start
  197.3 9.8 %fusion.32 = f32[32,512,128]{2,1,0:T(8,128)} fusion(bf16[256,32,512]{2,0,1:T(8,128)(2,1)} %get-tuple-element.24, bf16[256,128,32]{1,0,2:T(8,128)(2,1)} %copy.60), kind=kOutput, calls=%fused_computation.34 | convolution fusion | flops 1073741824 | bytes 18874368 | tf_op jit(solution)/shard_map/tjk,tbj->jkb/dot_general | solution.py:75
  207.1 0.0 reduce-scatter.9.cloned.1.call-update
  207.1 3.6 convolution_convert_fusion
  210.7 0.0 copy-start.7
  210.7 4.2 %copy.71 = bf16[256,4096]{1,0:T(8,128)(2,1)} copy(bf16[256,4096]{0,1:T(8,128)(2,1)} %bitcast.108) | data formatting | bytes 4194304
  214.9 0.0 copy-done.7
  214.9 3.7 convolution_convert_fusion.1
  218.6 4.1 copy.70
  222.7 0.0 reduce-scatter.5.cloned.1.call-done
  222.7 1.8 copy.72
  224.5 0.0 reduce-scatter.11.cloned.1.call-done
  224.5 89.2 %reduce-scatter.7.cloned.1.call-done = f32[32,16,512]{2,1,0:T(8,128)} async-done(((f32[32,128,512]{2,1,0:T(8,128)}), f32[32,16,512]{2,1,0:T(8,128)}) %reduce-scatter.7.cloned.1.call-update) | async-done | bytes 1048592 | tf_op jit(solution)/shard_map/reduce_scatter | solution.py:96
  313.7 90.7 %reduce-scatter.9.cloned.1.call-done = f32[32,64,128]{2,1,0:T(8,128)} async-done(((f32[32,512,128]{2,1,0:T(8,128)}), f32[32,64,128]{2,1,0:T(8,128)}) %reduce-scatter.9.cloned.1.call-update) | async-done | bytes 1048592 | tf_op jit(solution)/shard_map/reduce_scatter | solution.py:97
Async XLA Ops:
  7.2 9.6 %copy-start = (bf16[256,4096]{1,0:T(8,128)(2,1)S(1)}, bf16[256,4096]{1,0:T(8,128)(2,1)}, u32[]{:S(2)}) copy-start(bf16[256,4096]{1,0:T(8,128)(2,1)} %param.6) | copy-start | bytes 6291460
  11.5 5.3 %copy-start.6 = (bf16[32,128,128]{2,1,0:T(8,128)(2,1)S(1)}, bf16[32,128,128]{2,1,0:T(8,128)(2,1)}, u32[]{:S(2)}) copy-start(bf16[32,128,128]{2,1,0:T(8,128)(2,1)} %param.7) | copy-start | bytes 3145732
  11.5 31.1 %all-to-all-start.2 = ((bf16[256,4,1024]{0,2,1:T(8,128)(2,1)}), bf16[256,4,1024]{0,2,1:T(8,128)(2,1)}, u32[]{:S(2)}, u32[]{:S(2)}) async-start(bf16[256,4,1024]{0,2,1:T(8,128)(2,1)} %bitcast.103), calls=%async_computation.2 | async-start | bytes 4194304 | tf_op jit(solution)/shard_map/all_to_all | solution.py:72
  42.5 29.1 %all-to-all-start = ((bf16[256,4,1024]{0,2,1:T(8,128)(2,1)}), bf16[256,4,1024]{0,2,1:T(8,128)(2,1)}, u32[]{:S(2)}, u32[]{:S(2)}) async-start(bf16[256,4,1024]{0,2,1:T(8,128)(2,1)} %bitcast.102), calls=%async_computation | async-start | bytes 4194304 | tf_op jit(solution)/shard_map/all_to_all | solution.py:50
  47.1 175.6 %reduce-scatter.5.cloned.1.call-start = ((), (), s32[]{:S(2)}) async-start(), calls=%async_computation.8 | async-start | bytes 2359296 | tf_op jit(solution)/shard_map/reduce_scatter | solution.py:95
  71.7 14.1 %copy-start.4 = (bf16[256,128,32]{1,0,2:T(8,128)(2,1)S(1)}, bf16[256,128,32]{1,0,2:T(8,128)(2,1)}, u32[]{:S(2)}) copy-start(bf16[256,128,32]{1,0,2:T(8,128)(2,1)} %copy.60) | copy-start | bytes 6291460
  85.8 17.3 %copy-start.5 = (bf16[32,128,512]{2,1,0:T(8,128)(2,1)S(1)}, bf16[32,128,512]{2,1,0:T(8,128)(2,1)}, u32[]{:S(2)}) copy-start(bf16[32,128,512]{2,1,0:T(8,128)(2,1)} %param.8) | copy-start | bytes 12582916
  138.2 1.4 copy-start.1
  144.8 79.7 %reduce-scatter.11.cloned.1.call-start = ((), (), s32[]{:S(2)}) async-start(), calls=%async_computation.11 | async-start | bytes 2359296 | tf_op jit(solution)/shard_map/reduce_scatter | solution.py:98
  182.4 2.3 copy-start.3
  182.6 1.3 copy-start.2
  186.8 126.9 %reduce-scatter.7.cloned.1.call-start = ((), (), s32[]{:S(2)}) async-start(), calls=%async_computation.9 | async-start | bytes 9437184 | tf_op jit(solution)/shard_map/reduce_scatter | solution.py:96
  197.0 207.4 %reduce-scatter.9.cloned.1.call-start = ((), (), s32[]{:S(2)}) async-start(), calls=%async_computation.10 | async-start | bytes 9437184 | tf_op jit(solution)/shard_map/reduce_scatter | solution.py:97
  210.7 4.2 %copy-start.7 = (bf16[32,128,128]{2,1,0:T(8,128)(2,1)S(1)}, bf16[32,128,128]{2,1,0:T(8,128)(2,1)}, u32[]{:S(2)}) copy-start(bf16[32,128,128]{2,1,0:T(8,128)(2,1)} %param.10) | copy-start | bytes 3145732
Sparse Core Ops, SparseCore 0:
  144.9 35.9 reduce-scatter.4
  186.9 35.7 reduce-scatter.10
  225.6 88.0 reduce-scatter.6
  316.4 87.9 reduce-scatter.8
where the time goes:
time: 412 us; the launch traced here: 411 us
  waiting for transfers between devices  224 us (54%)
  matrix products  81.3 us (20%)
  blocking collectives  53.4 us (13%)
  local copies, waits for them, and re-layouts  28.7 us (7%)
  between operations  13.9 us (3%)
  starting transfers between devices  10.2 us (2%)
    reduce_scatter x1, waiting for transfers between devices, local(): lax.psum_scatter(g_fd, 'dp', scatter_dimension=1, tiled=True)  90.7 us
    reduce_scatter x1, waiting for transfers between devices, local(): lax.psum_scatter(g_su, 'dp', scatter_dimension=1, tiled=True)  89.2 us
    all_to_all x1, blocking collectives, local(): lax.all_to_all(back_in_j.reshape(count, groups, -1), 'block', split_axis=...  27.4 us
    all_to_all x1, blocking collectives, local(): lax.all_to_all(out_j.reshape(count, groups, -1), 'block', split_axis=1, c...  26 us
    all_to_all x1, waiting for transfers between devices, local(): lax.all_to_all(pack_blocks(back_out, groups), 'block', split_axis=1, conc...  23.4 us
    all_to_all x1, waiting for transfers between devices, local(): lax.all_to_all(packed_in, 'block', split_axis=1, concat_axis=1, tiled=True)  20.1 us
    dot_general x1, matrix products, local(): jnp.einsum('tbj,jkb->tjk', back_j, first_down, preferred_element_type=wide)  17.3 us
    dot_general x1, matrix products, local(): jnp.einsum('tbj,jbk->tjk', mixed_piece, second_up, preferred_element_type...  14.1 us
  transfers between devices with their start and end apart: 6, of which 4 were waited for; matrix products, arithmetic and copies ran while one was open for 14% of the time, Pallas kernels for 0%

commit v1 on v0

--- a/solution.py
+++ b/solution.py
@@ -3,6 +3,22 @@
 import jax.numpy as jnp
 from jax import lax
 from jax.sharding import PartitionSpec as P
+
+
+def exchange_in_pairs(array, axis, split, join):
+    ways, here = (lax.axis_size(axis), lax.axis_index(axis))
+    width = array.shape[split] // ways
+    shape = list(array.shape)
+    shape[split] = width
+    height = shape[join]
+    shape[join] = height * ways
+    full = jnp.zeros(shape, array.dtype)
+    for mask in range(ways):
+        part = lax.dynamic_slice_in_dim(array, (here ^ mask) * width, width, axis=split)
+        if mask:
+            part = lax.ppermute(part, axis, [(d, d ^ mask) for d in range(ways)])
+        full = lax.dynamic_update_slice_in_dim(full, part, (here ^ mask) * height, axis=join)
+    return full
 
 
 def gelu_pair(values):
@@ -47,7 +63,7 @@
         narrow
     )
     packed_in = pack_blocks(mixed_in, groups)
-    piece = lax.all_to_all(packed_in, "block", split_axis=1, concat_axis=1, tiled=True)
+    piece = exchange_in_pairs(packed_in, "block", 1, 1)
     mixed_piece = piece.reshape(piece.shape[0], -1, local_feats)
     before = jnp.einsum("tbj,jbk->tjk", mixed_piece, second_up, preferred_element_type=wide)
     active, slope_term = gelu_pair(before)

time: 412 us -> 397 us (0.964)
  waiting for transfers between devices: 224 us -> 204 us
  local copies, waits for them, and re-layouts: 28.7 us -> 39.5 us
  blocking collectives: 53.4 us -> 47.7 us
    ppermute x0 -> x3, waiting for transfers between devices: none -> 27.4 us  [exchange_in_pairs(): part = lax.ppermute(part, axis, [(d, d ^ mask) for d in range(ways)])]
    all_to_all x1, waiting for transfers between devices: 23.4 us -> 0.01 us  [local(): lax.all_to_all(pack_blocks(back_out, groups), 'block', split_axis=1, conc...]
    all_to_all x1 -> x0, waiting for transfers between devices: 20.1 us -> none  [local(): lax.all_to_all(packed_in, 'block', split_axis=1, concat_axis=1, tiled=True)]
    dynamic_update_slice x0 -> x3, local copies, waits for them, and re-layouts: none -> 5.6 us  [exchange_in_pairs(): lax.dynamic_update_slice_in_dim(full, part, (here ^ mask) * height, axis=...]
    all_to_all x1 -> x0, starting transfers between devices: 4.51 us -> none  [local(): lax.all_to_all(packed_in, 'block', split_axis=1, concat_axis=1, tiled=True)]
    ppermute x0 -> x3, starting transfers between devices: none -> 4.48 us  [exchange_in_pairs(): part = lax.ppermute(part, axis, [(d, d ^ mask) for d in range(ways)])]
    unnamed x19 -> x21, local copies, waits for them, and re-layouts: 13.5 us -> 16 us
  transfers between devices with their start and end apart: 6 -> 8, of which waited for: 4 -> 4; matrix products, arithmetic and copies ran while one was open for 14% -> 19% of each run, Pallas kernels for 0% -> 0%
where the time goes in v1:
time: 397 us; the launch traced here: 396 us
  waiting for transfers between devices  204 us (51%)
  matrix products  81.1 us (20%)
  blocking collectives  47.7 us (12%)
  local copies, waits for them, and re-layouts  39.5 us (10%)
  between operations  13.9 us (4%)
  starting transfers between devices  9.39 us (2%)
    reduce_scatter x1, waiting for transfers between devices, local(): lax.psum_scatter(g_fd, 'dp', scatter_dimension=1, tiled=True)  90.7 us
    reduce_scatter x1, waiting for transfers between devices, local(): lax.psum_scatter(g_su, 'dp', scatter_dimension=1, tiled=True)  86 us
    ppermute x3, waiting for transfers between devices, exchange_in_pairs(): part = lax.ppermute(part, axis, [(d, d ^ mask) for d in range(ways)])  27.4 us
    all_to_all x1, blocking collectives, local(): lax.all_to_all(back_in_j.reshape(count, groups, -1), 'block', split_axis=...  24.8 us
    all_to_all x1, blocking collectives, local(): lax.all_to_all(out_j.reshape(count, groups, -1), 'block', split_axis=1, c...  22.9 us
    dot_general x1, matrix products, local(): jnp.einsum('tbj,jkb->tjk', back_j, first_down, preferred_element_type=wide)  17.6 us
    unnamed x21, local copies, waits for them, and re-layouts  16 us
    dot_general x1, matrix products, local(): jnp.einsum('tbj,jbk->tjk', mixed_piece, second_up, preferred_element_type...  14 us
  transfers between devices with their start and end apart: 8, of which 4 were waited for; matrix products, arithmetic and copies ran while one was open for 19% of the time, Pallas kernels for 0%

profile of v1, /device:TPU:0, one launch (start us, length us, event | category | flops | bytes accessed | tf_op | source)
XLA Modules:
  0.0 395.8 jit_solution(7982508702001988780)
XLA Ops:
  7.2 0.0 copy-start
  7.2 1.6 copy-done
  8.8 2.0 fusion.15
  10.7 1.5 copy.51
  12.3 0.0 copy-start.5
  12.3 1.5 broadcast_in_dim.3
  13.7 0.9 copy-done.5
  14.6 0.0 copy-start.3
  14.6 0.0 copy-start.7
  14.6 1.3 constant_dynamic-slice_fusion
  16.0 3.0 collective-permute-start
  19.0 1.5 collective-permute-start.1
  20.5 0.0 collective-permute-start.2
  20.5 0.0 copy-done.3
  20.5 0.0 copy-done.7
  20.5 0.7 fusion.18
  21.2 1.5 copy.59
  22.7 4.5 %all-to-all-start.1 = ((bf16[256,4,1024]{0,2,1:T(8,128)(2,1)}), bf16[256,4,1024]{0,2,1:T(8,128)(2,1)}, u32[]{:S(2)}, u32[]{:S(2)}) async-start(bf16[256,4,1024]{0,2,1:T(8,128)(2,1)} %bitcast.102), calls=%async_computation.1 | async-start | bytes 4194304 | tf_op jit(solution)/shard_map/all_to_all | solution.py:88
  27.2 0.0 reduce-scatter.5.cloned.1.call-start
  27.3 4.8 %collective-permute-done = bf16[256,1,1024]{0,2,1:T(8,128)(2,1)} collective-permute-done((bf16[256,1,1024]{0,2,1:T(8,128)(2,1)}, bf16[256,1,1024]{0,2,1:T(8,128)(2,1)}, u32[]{:S(2)}, u32[]{:S(2)}) %collective-permute-start) | collective-permute-done | bytes 524320 | tf_op jit(solution)/shard_map/ppermute | solution.py:19
  32.0 1.9 constant_dynamic-update-slice_fusion.1
  33.9 22.6 %collective-permute-done.1 = bf16[256,1,1024]{0,2,1:T(8,128)(2,1)} collective-permute-done((bf16[256,1,1024]{0,2,1:T(8,128)(2,1)}, bf16[256,1,1024]{0,2,1:T(8,128)(2,1)}, u32[]{:S(2)}, u32[]{:S(2)}) %collective-permute-start.1) | collective-permute-done | bytes 524320 | tf_op jit(solution)/shard_map/ppermute | solution.py:19
  56.5 1.9 constant_dynamic-update-slice_fusion
  58.4 0.0 collective-permute-done.2
  58.4 1.9 constant_dynamic-update-slice_fusion.2
  60.3 14.0 %multiply_convert_fusion = (bf16[256,32,512]{2,0,1:T(8,128)(2,1)}, f32[32,256,512]{2,1,0:T(8,128)}) fusion(bf16[32,128,512]{2,1,0:T(8,128)(2,1)} %param.8, bf16[256,128,32]{0,2,1:T(8,128)(2,1)} %bitcast.5), kind=kOutput, calls=%fused_computation.10 | convolution fusion | flops 1111490560 | bytes 31457280 | tf_op jit(solution)/shard_map/tbj,jbk->tjk/dot_general | solution.py:68
  74.2 0.0 all-to-all-done.1
  74.2 4.5 %copy.60 = bf16[256,128,32]{1,0,2:T(8,128)(2,1)} copy(bf16[256,128,32]{0,2,1:T(8,128)(2,1)} %bitcast.18) | data formatting | bytes 4194304 | tf_op jit(solution)/shard_map/reshape | solution.py:90
  78.8 0.0 copy-start.6
  78.8 17.6 %fusion.6 = bf16[256,32,512]{2,0,1:T(8,128)(2,1)} fusion(f32[32,256,512]{2,1,0:T(8,128)} %get-tuple-element.29, bf16[256,128,32]{1,0,2:T(8,128)(2,1)} %copy.60, bf16[32,512,128]{2,1,0:T(8,128)(2,1)} %param.9), kind=kOutput, calls=%fused_computation.8 | convolution fusion | flops 1153433600 | bytes 31457280 | tf_op jit(solution)/shard_map/tbj,jkb->tjk/dot_general | solution.py:93
  96.4 0.0 copy-done.6
  96.4 6.3 %convert_bitcast_fusion = bf16[256,128,32]{0,1,2:T(8,128)(2,1)S(1)} fusion(bf16[256,32,512]{2,0,1:T(8,128)(2,1)} %fusion.6, bf16[32,128,512]{2,1,0:T(8,128)(2,1)S(1)} %copy-done.6), kind=kOutput, calls=%fused_computation.19 | convolution fusion | flops 1074790400 | bytes 14680064 | tf_op jit(solution)/shard_map/tjk,jbk->tbj/dot_general | solution.py:96
  102.6 1.2 copy.61
  103.8 24.8 %all_to_all.15 = bf16[256,4,1024]{0,2,1:T(8,128)(2,1)S(1)} all-to-all(bf16[256,4,1024]{0,2,1:T(8,128)(2,1)S(1)} %bitcast.104), channel_id=1, replica_groups=mesh['block'=4,'dp'=8] {'block'}, dimensions={1} | all-to-all | bytes 4194304 | tf_op jit(solution)/shard_map/all_to_all | solution.py:100
  128.7 0.2 copy.62
  128.9 0.0 copy-start.1
  128.9 1.3 copy-done.1
  130.2 2.1 fusion.29
  132.3 3.1 copy.65
  135.4 0.0 reduce-scatter.5.cloned.1.call-update
  135.4 0.0 reduce-scatter.11.cloned.1.call-start
  135.5 9.0 %convert_bitcast_fusion.1 = bf16[256,128,32]{0,1,2:T(8,128)(2,1)} fusion(bf16[256,32,512]{2,0,1:T(8,128)(2,1)} %get-tuple-element.28, bf16[32,512,128]{2,1,0:T(8,128)(2,1)} %param.9), kind=kOutput, calls=%fused_computation.20 | convolution fusion | flops 1074790400 | bytes 14680064 | tf_op jit(solution)/shard_map/tjk,jkb->tbj/dot_general | solution.py:71
  144.5 2.8 copy.54
  147.3 22.9 %all_to_all.16 = bf16[256,4,1024]{0,2,1:T(8,128)(2,1)S(1)} all-to-all(bf16[256,4,1024]{0,2,1:T(8,128)(2,1)S(1)} %bitcast.106), channel_id=1, replica_groups=mesh['block'=4,'dp'=8] {'block'}, dimensions={1} | all-to-all | bytes 4194304 | tf_op jit(solution)/shard_map/all_to_all | solution.py:75
  170.1 0.2 copy.55
  170.4 0.0 copy-start.2
  170.4 1.3 copy-done.2
  171.7 0.8 copy-done.4
  172.5 2.1 fusion.7
  174.5 0.0 reduce-scatter.11.cloned.1.call-update
  174.6 0.0 reduce-scatter.7.cloned.1.call-start
  174.6 10.4 %fusion.27 = f32[32,128,512]{2,1,0:T(8,128)} fusion(bf16[256,32,512]{2,0,1:T(8,128)(2,1)} %fusion.6, bf16[256,128,32]{0,2,1:T(8,128)(2,1)} %bitcast.5), kind=kOutput, calls=%fused_computation.31 | convolution fusion | flops 1073741824 | bytes 18874368 | tf_op jit(solution)/shard_map/tbj,tjk->jbk/dot_general | solution.py:95
  185.0 0.0 reduce-scatter.7.cloned.1.call-update
  185.0 0.3 reduce-scatter.9.cloned.1.call-start
  185.3 9.8 %fusion.32 = f32[32,512,128]{2,1,0:T(8,128)} fusion(bf16[256,32,512]{2,0,1:T(8,128)(2,1)} %get-tuple-element.28, bf16[256,128,32]{1,0,2:T(8,128)(2,1)} %copy.60), kind=kOutput, calls=%fused_computation.41 | convolution fusion | flops 1073741824 | bytes 18874368 | tf_op jit(solution)/shard_map/tjk,tbj->jkb/dot_general | solution.py:91
  195.1 0.0 reduce-scatter.9.cloned.1.call-update
  195.1 3.7 convolution_convert_fusion.1
  198.8 4.2 %copy.70 = bf16[256,4096]{1,0:T(8,128)(2,1)} copy(bf16[256,4096]{0,1:T(8,128)(2,1)} %bitcast.108) | data formatting | bytes 4194304
  203.0 0.0 copy-done.8
  203.0 3.6 convolution_convert_fusion
  206.6 4.1 %copy.71 = bf16[256,4096]{1,0:T(8,128)(2,1)} copy(bf16[256,4096]{0,1:T(8,128)(2,1)} %bitcast.109) | data formatting | bytes 4194304
  210.7 1.8 copy.72
  212.5 86.0 %reduce-scatter.7.cloned.1.call-done = f32[32,16,512]{2,1,0:T(8,128)} async-done(((f32[32,128,512]{2,1,0:T(8,128)}), f32[32,16,512]{2,1,0:T(8,128)}) %reduce-scatter.7.cloned.1.call-update) | async-done | bytes 1048592 | tf_op jit(solution)/shard_map/reduce_scatter | solution.py:112
  298.5 90.7 %reduce-scatter.9.cloned.1.call-done = f32[32,64,128]{2,1,0:T(8,128)} async-done(((f32[32,512,128]{2,1,0:T(8,128)}), f32[32,64,128]{2,1,0:T(8,128)}) %reduce-scatter.9.cloned.1.call-update) | async-done | bytes 1048592 | tf_op jit(solution)/shard_map/reduce_scatter | solution.py:113
  (4 shorter events, 0.0 us)
Async XLA Ops:
  7.2 1.6 copy-start
  12.3 2.3 copy-start.5
  14.6 5.8 %copy-start.3 = (bf16[256,4096]{1,0:T(8,128)(2,1)S(1)}, bf16[256,4096]{1,0:T(8,128)(2,1)}, u32[]{:S(2)}) copy-start(bf16[256,4096]{1,0:T(8,128)(2,1)} %param.11) | copy-start | bytes 6291460
  14.6 5.8 %copy-start.7 = (bf16[32,128,128]{2,1,0:T(8,128)(2,1)S(1)}, bf16[32,128,128]{2,1,0:T(8,128)(2,1)}, u32[]{:S(2)}) copy-start(bf16[32,128,128]{2,1,0:T(8,128)(2,1)} %param.10) | copy-start | bytes 3145732
  16.0 16.1 %collective-permute-start = (bf16[256,1,1024]{0,2,1:T(8,128)(2,1)}, bf16[256,1,1024]{0,2,1:T(8,128)(2,1)}, u32[]{:S(2)}, u32[]{:S(2)}) collective-permute-start(bf16[256,1,1024]{0,2,1:T(8,128)(2,1)} %get-tuple-element.26), channel_id=1, source_target_pairs={{0,8},{8,0},{16,24},{24,16},{1,9},{9,1},{17,25},{25,17},{2,10},{10... | collective-permute-start | bytes 1572872 | tf_op jit(solution)/shard_map/ppermute | solution.py:19
  19.0 37.6 %collective-permute-start.1 = (bf16[256,1,1024]{0,2,1:T(8,128)(2,1)}, bf16[256,1,1024]{0,2,1:T(8,128)(2,1)}, u32[]{:S(2)}, u32[]{:S(2)}) collective-permute-start(bf16[256,1,1024]{0,2,1:T(8,128)(2,1)} %get-tuple-element.25), channel_id=1, source_target_pairs={{0,16},{8,24},{16,0},{24,8},{1,17},{9,25},{17,1},{25,9},{2,18},{10... | collective-permute-start | bytes 1572872 | tf_op jit(solution)/shard_map/ppermute | solution.py:19
  20.5 37.9 %collective-permute-start.2 = (bf16[256,1,1024]{0,2,1:T(8,128)(2,1)}, bf16[256,1,1024]{0,2,1:T(8,128)(2,1)}, u32[]{:S(2)}, u32[]{:S(2)}) collective-permute-start(bf16[256,1,1024]{0,2,1:T(8,128)(2,1)} %get-tuple-element.24), channel_id=1, source_target_pairs={{0,24},{8,16},{16,8},{24,0},{1,25},{9,17},{17,9},{25,1},{2,26},{10... | collective-permute-start | bytes 1572872 | tf_op jit(solution)/shard_map/ppermute | solution.py:19
  22.7 51.5 %all-to-all-start.1 = ((bf16[256,4,1024]{0,2,1:T(8,128)(2,1)}), bf16[256,4,1024]{0,2,1:T(8,128)(2,1)}, u32[]{:S(2)}, u32[]{:S(2)}) async-start(bf16[256,4,1024]{0,2,1:T(8,128)(2,1)} %bitcast.102), calls=%async_computation.1 | async-start | bytes 4194304 | tf_op jit(solution)/shard_map/all_to_all | solution.py:88
  27.2 183.4 %reduce-scatter.5.cloned.1.call-start = ((), (), s32[]{:S(2)}) async-start(), calls=%async_computation.7 | async-start | bytes 2359296 | tf_op jit(solution)/shard_map/reduce_scatter | solution.py:111
  78.8 17.6 %copy-start.6 = (bf16[32,128,512]{2,1,0:T(8,128)(2,1)S(1)}, bf16[32,128,512]{2,1,0:T(8,128)(2,1)}, u32[]{:S(2)}) copy-start(bf16[32,128,512]{2,1,0:T(8,128)(2,1)} %param.8) | copy-start | bytes 12582916
  128.9 1.4 copy-start.1
  135.4 77.1 %reduce-scatter.11.cloned.1.call-start = ((), (), s32[]{:S(2)}) async-start(), calls=%async_computation.10 | async-start | bytes 2359296 | tf_op jit(solution)/shard_map/reduce_scatter | solution.py:114
  170.1 2.3 copy-start.4
  170.4 1.3 copy-start.2
  174.6 123.9 %reduce-scatter.7.cloned.1.call-start = ((), (), s32[]{:S(2)}) async-start(), calls=%async_computation.8 | async-start | bytes 9437184 | tf_op jit(solution)/shard_map/reduce_scatter | solution.py:112
  185.0 204.2 %reduce-scatter.9.cloned.1.call-start = ((), (), s32[]{:S(2)}) async-start(), calls=%async_computation.9 | async-start | bytes 9437184 | tf_op jit(solution)/shard_map/reduce_scatter | solution.py:113
  198.8 4.2 %copy-start.8 = (bf16[32,128,128]{2,1,0:T(8,128)(2,1)S(1)}, bf16[32,128,128]{2,1,0:T(8,128)(2,1)}, u32[]{:S(2)}) copy-start(bf16[32,128,128]{2,1,0:T(8,128)(2,1)} %param.7) | copy-start | bytes 3145732
Sparse Core Ops, SparseCore 0:
  135.5 32.7 reduce-scatter.4
  174.7 32.5 reduce-scatter.10
  210.2 88.2 reduce-scatter.6
  301.2 87.9 reduce-scatter.8
